TPU v7x, 512 devices: a whole 4x4x16 slice. The times are simulated.
512 devices in a mesh: dp: 32 (over y_lo, z), gx: 2 (over core), gy: 8 (over x, y_hi).
Axes of the slice: x: 4, y: 4 (y_hi: 2, y_lo: 2; y = y_hi * 2 + y_lo), z: 16, core: 2. Of those that a mesh axis runs over, the one named last changes fastest.
Arguments:
- field: float32 [32, 64, 1024], P('dp', 'gx', 'gy'), may hold values from -6 to 6
- cotangent: float32 [32, 64, 1024], P('dp', 'gx', 'gy')
- checker: int32 [64, 1024], P('gx', 'gy'), may hold values from 0 to 1, as said below
- weight_in: float32 [3, 3, 32], replicated, may hold values from -2 to 2
- weight_mid: bfloat16 [3, 3, 32, 32], replicated, may hold values from -0.375 to 0.375
- weight_head: bfloat16 [2, 32], replicated, may hold values from -1 to 1
- prior_grads: float32 [32, 2, 8, 23, 9568], P('dp', 'gx', 'gy')
Outputs:
- coupled: float32 [32, 64, 1024], P('dp', 'gx', 'gy')
- field_grad: float32 [32, 64, 1024], P('dp', 'gx', 'gy')
- summed_grads: float32 [24, 9568], replicated
Inputs may be any that keep to these rules, and one draw needn't show every extreme that they name: Each row alternates along the columns: checker[i, j] = (j + p[i]) mod 2, with a parity p[i] of its own for every row i.
All inputs are finite; a program needn't handle non-finite values.
Results may differ from a plain program's by a relative error of at most 0.0034.
Values may be sent and summed in bfloat16 or wider, within the bound.
A program may use at most 64 MiB of HBM per device.

v0:
```python
import math
import jax
import jax.numpy as jnp
from jax import lax
from jax.sharding import PartitionSpec as P


def extended(value, sides, width):
    for axis, dim in sides:
        size, length = (lax.axis_size(axis), value.shape[dim])
        up = [(i, (i + 1) % size) for i in range(size)]
        down = [(j, i) for i, j in up]
        last = lax.slice_in_dim(value, length - width, length, axis=dim)
        initial = lax.slice_in_dim(value, 0, width, axis=dim)
        before = lax.ppermute(last, axis, up)
        after = lax.ppermute(initial, axis, down)
        value = jnp.concatenate([before, value, after], axis=dim)
    return value


def first_conv(padded, weight_in, row_count, col_count):
    total = jnp.zeros((weight_in.shape[2], row_count, col_count), jnp.float32)
    for row_tap in range(3):
        for col_tap in range(3):
            window = padded[row_tap : row_tap + row_count, col_tap : col_tap + col_count]
            total = total + weight_in[row_tap, col_tap][:, None, None] * window[None]
    return total


def on_device(field, cotangent, checker, weight_in, weight_mid, weight_head, prior_grads):
    highest = lax.Precision.HIGHEST
    row_count = field.shape[1]
    col_count = field.shape[2]
    hidden_width = weight_mid.shape[2]
    cell_total = (
        lax.axis_size("dp") * row_count * lax.axis_size("gx") * col_count * lax.axis_size("gy")
    )
    grad_scale = 1.0 / math.sqrt(cell_total)
    values = field[0]
    downstream = cotangent[0]
    frozen = checker.astype(jnp.float32)
    unfrozen = 1.0 - frozen
    masked = frozen * values
    partial_prior = prior_grads.reshape(prior_grads.shape[3], prior_grads.shape[4])
    padded_field = extended(masked, (("gx", 0), ("gy", 1)), 1)
    hidden_one = jnp.tanh(first_conv(padded_field, weight_in, row_count, col_count)).astype(
        jnp.bfloat16
    )
    hidden_pad = extended(hidden_one, (("gx", 1), ("gy", 2)), 1)
    hidden_inner = hidden_pad[:, 1:-1, 1:-1]
    pre_two = jnp.zeros((hidden_width, row_count, col_count), jnp.float32)
    for row_tap in range(3):
        for col_tap in range(3):
            window = hidden_pad[:, row_tap : row_tap + row_count, col_tap : col_tap + col_count]
            pre_two = pre_two + jnp.einsum(
                "oc,cxy->oxy",
                weight_mid[row_tap, col_tap],
                window,
                preferred_element_type=jnp.float32,
            )
    hidden_two = jnp.tanh(pre_two).astype(jnp.bfloat16)
    pair = jnp.einsum("ko,oxy->kxy", weight_head, hidden_two, preferred_element_type=jnp.float32)
    expo = jnp.exp(pair[0])
    coupled = masked + unfrozen * (values * expo + pair[1])
    d_pair = jnp.stack([unfrozen * downstream * values * expo, unfrozen * downstream]).astype(
        jnp.bfloat16
    )
    grad_head = jnp.einsum("kxy,oxy->ko", d_pair, hidden_two, preferred_element_type=jnp.float32)
    d_hidden_two = jnp.einsum(
        "ko,kxy->oxy", weight_head, d_pair, preferred_element_type=jnp.float32
    )
    two_f = hidden_two.astype(jnp.float32)
    d_pre_two = (d_hidden_two * (1.0 - two_f * two_f)).astype(jnp.bfloat16)
    d_two_pad = extended(d_pre_two, (("gx", 1), ("gy", 2)), 1)
    mid_list = []
    d_hidden_one = jnp.zeros((hidden_width, row_count, col_count), jnp.float32)
    for row_tap in range(3):
        for col_tap in range(3):
            window = hidden_pad[:, row_tap : row_tap + row_count, col_tap : col_tap + col_count]
            mid_list.append(
                jnp.einsum("oxy,cxy->oc", d_pre_two, window, preferred_element_type=jnp.float32)
            )
            back_window = d_two_pad[
                :, 2 - row_tap : 2 - row_tap + row_count, 2 - col_tap : 2 - col_tap + col_count
            ]
            d_hidden_one = d_hidden_one + jnp.einsum(
                "oc,oxy->cxy",
                weight_mid[row_tap, col_tap],
                back_window,
                preferred_element_type=jnp.float32,
            )
    one_f = hidden_inner.astype(jnp.float32)
    d_pre_one = d_hidden_one * (1.0 - one_f * one_f)
    in_list = []
    for row_tap in range(3):
        for col_tap in range(3):
            window = padded_field[row_tap : row_tap + row_count, col_tap : col_tap + col_count]
            in_list.append(jnp.einsum("oxy,xy->o", d_pre_one, window, precision=highest))
    d_one_pad = extended(d_pre_one, (("gx", 1), ("gy", 2)), 1)
    d_masked = jnp.zeros((row_count, col_count), jnp.float32)
    for row_tap in range(3):
        for col_tap in range(3):
            back_window = d_one_pad[
                :, 2 - row_tap : 2 - row_tap + row_count, 2 - col_tap : 2 - col_tap + col_count
            ]
            d_masked = d_masked + jnp.einsum(
                "o,oxy->xy", weight_in[row_tap, col_tap], back_window, precision=highest
            )
    field_grad = frozen * downstream + unfrozen * downstream * expo + frozen * d_masked
    layer_grads = (
        jnp.concatenate(
            [jnp.stack(in_list).reshape(-1), jnp.stack(mid_list).reshape(-1), grad_head.reshape(-1)]
        )
        * grad_scale
    )
    stacked = jnp.concatenate([layer_grads[None], partial_prior], axis=0)
    summed_grads = lax.psum(stacked, ("dp", "gx", "gy"))
    return (coupled[None], field_grad[None], summed_grads)


def solution(mesh):
    placed = (
        P("dp", "gx", "gy"),
        P("dp", "gx", "gy"),
        P("gx", "gy"),
        P(),
        P(),
        P(),
        P("dp", "gx", "gy", None, None),
    )
    return jax.shard_map(
        on_device,
        mesh=mesh,
        in_specs=placed,
        out_specs=(P("dp", "gx", "gy"), P("dp", "gx", "gy"), P()),
        check_vma=False,
    )
```

profile of v0, /device:TPU:1, one launch (start us, length us, event | category | flops | bytes accessed | tf_op | source)
XLA Modules:
  0.0 572.6 jit_solution(7181842597088774773)
XLA Ops:
  7.2 0.7 bitcast_multiply_fusion.6
  8.0 8.8 %collective-permute-start = (f32[1,128]{1,0:T(1,128)S(1)}, f32[1,128]{1,0:T(1,128)S(1)}, u32[]{:S(2)}, u32[]{:S(2)}) collective-permute-start(f32[1,128]{1,0:T(1,128)S(1)} %get-tuple-element.38), channel_id=1, source_target_pairs={{0,8},{8,0},{1,9},{9,1},{2,10},{10,2},{3,11},{11,3},{4,12},{12,4},... | collective-permute-start | bytes 1544 | tf_op jit(solution)/shard_map/ppermute | solution.py:15
  16.8 1.9 collective-permute-start.1
  18.7 0.8 slice_bitcast_fusion.8
  19.6 1.3 copy.81
  20.9 1.9 collective-permute-start.2
  22.9 7.0 %collective-permute-start.3 = (f32[34,1]{1,0:T(8,128)S(1)}, f32[34,1]{1,0:T(8,128)S(1)}, u32[]{:S(2)}, u32[]{:S(2)}) collective-permute-start(f32[34,1]{1,0:T(8,128)S(1)} %get-tuple-element.33), channel_id=1, source_target_pairs={{1,0},{2,1},{3,2},{4,3},{5,4},{6,5},{7,6},{0,7},{9,8},{10,9},{11,1... | collective-permute-start | bytes 416 | tf_op jit(solution)/shard_map/ppermute | solution.py:16
  29.9 0.9 collective-permute-done.3
  31.3 3.5 collective-permute-start.4
  34.9 1.9 collective-permute-start.5
  37.0 0.9 collective-permute-done.5
  38.1 1.9 collective-permute-start.6
  40.0 7.5 %collective-permute-start.7 = (bf16[32,34,1]{2,0,1:T(8,128)(2,1)S(1)}, bf16[32,34,1]{2,0,1:T(8,128)(2,1)S(1)}, u32[]{:S(2)}, u32[]{:S(2)}) collective-permute-start(bf16[32,34,1]{2,0,1:T(8,128)(2,1)S(1)} %get-tuple-element.16), channel_id=1, source_target_pairs={{1,0},{2,1},{3,2},{4,3},{5,4},{6,5},{7,6},{0,7},{9,8},{10,9},{11,1... | collective-permute-start | bytes 6536 | tf_op jit(solution)/shard_map/ppermute | solution.py:16
  48.0 4.6 collective-permute-done.6
  52.7 4.9 collective-permute-done.7
  60.0 0.6 fusion.96
  63.3 2.9 collective-permute-start.9
  66.1 1.9 collective-permute-start.8
  68.5 0.7 collective-permute-done.8
  69.4 5.6 collective-permute-start.10
  75.0 1.9 collective-permute-start.11
  77.5 3.5 collective-permute-done.10
  81.0 7.4 %collective-permute-done.11 = bf16[32,34,1]{2,0,1:T(8,128)(2,1)S(1)} collective-permute-done((bf16[32,34,1]{2,0,1:T(8,128)(2,1)S(1)}, bf16[32,34,1]{2,0,1:T(8,128)(2,1)S(1)}, u32[]{:S(2)}, u32[]{:S(2)}) %collective-permute-start.11) | collective-permute-done | bytes 2208 | tf_op jit(solution)/shard_map/ppermute | solution.py:15
  95.8 3.2 collective-permute-start.13
  99.0 1.9 collective-permute-start.12
  100.9 1.0 pad_maximum_fusion.1
  103.1 6.0 %collective-permute-start.14 = (f32[32,34,1]{1,0,2:T(8,128)S(1)}, f32[32,34,1]{1,0,2:T(8,128)S(1)}, u32[]{:S(2)}, u32[]{:S(2)}) collective-permute-start(f32[32,34,1]{1,0,2:T(8,128)S(1)} %copy.33), channel_id=1, source_target_pairs={{1,0},{2,1},{3,2},{4,3},{5,4},{6,5},{7,6},{0,7},{9,8},{10,9},{11,1... | collective-permute-start | bytes 13064 | tf_op jit(solution)/shard_map/ppermute | solution.py:16
  109.5 1.9 collective-permute-start.15
  112.8 4.7 collective-permute-done.15
  121.3 0.6 fusion.86
  121.9 441.7 %all-reduce.2.cloned.1.call-done = f32[24,9568]{1,0:T(8,128)} async-done(((f32[24,9568]{1,0:T(8,128)}), f32[24,9568]{1,0:T(8,128)}) %all-reduce.2.cloned.1.call-update) | async-done | bytes 918544 | tf_op jit(solution)/shard_map/psum | solution.py:117
  563.6 2.2 copy.91
  (101 shorter events, 21.6 us)
Async XLA Ops:
  7.2 52.4 %copy-start = (bf16[2,32]{1,0:T(2,128)(2,1)S(1)}, bf16[2,32]{1,0:T(2,128)(2,1)}, u32[]{:S(2)}) copy-start(bf16[2,32]{1,0:T(2,128)(2,1)} %param.12) | copy-start | bytes 388
  7.2 556.4 %all-reduce.2.cloned.1.call-start = ((), (), s32[]{:S(2)}) async-start(), calls=%async_computation | async-start | bytes 1843200 | tf_op jit(solution)/shard_map/psum | solution.py:117
  8.0 12.9 %collective-permute-start = (f32[1,128]{1,0:T(1,128)S(1)}, f32[1,128]{1,0:T(1,128)S(1)}, u32[]{:S(2)}, u32[]{:S(2)}) collective-permute-start(f32[1,128]{1,0:T(1,128)S(1)} %get-tuple-element.38), channel_id=1, source_target_pairs={{0,8},{8,0},{1,9},{9,1},{2,10},{10,2},{3,11},{11,3},{4,12},{12,4},... | collective-permute-start | bytes 1544 | tf_op jit(solution)/shard_map/ppermute | solution.py:15
  16.8 4.1 collective-permute-start.1
  19.5 17.2 %copy-start.1 = (bf16[3,3,32,32]{3,2,1,0:T(8,128)(2,1)S(1)}, bf16[3,3,32,32]{3,2,1,0:T(8,128)(2,1)}, u32[]{:S(2)}) copy-start(bf16[3,3,32,32]{3,2,1,0:T(8,128)(2,1)} %param.11) | copy-start | bytes 55300
  20.9 8.9 %collective-permute-start.2 = (f32[34,1]{1,0:T(8,128)S(1)}, f32[34,1]{1,0:T(8,128)S(1)}, u32[]{:S(2)}, u32[]{:S(2)}) collective-permute-start(f32[34,1]{1,0:T(8,128)S(1)} %get-tuple-element.32), channel_id=1, source_target_pairs={{0,1},{1,2},{2,3},{3,4},{4,5},{5,6},{6,7},{7,0},{8,9},{9,10},{10,1... | collective-permute-start | bytes 416 | tf_op jit(solution)/shard_map/ppermute | solution.py:15
  22.9 7.9 %collective-permute-start.3 = (f32[34,1]{1,0:T(8,128)S(1)}, f32[34,1]{1,0:T(8,128)S(1)}, u32[]{:S(2)}, u32[]{:S(2)}) collective-permute-start(f32[34,1]{1,0:T(8,128)S(1)} %get-tuple-element.33), channel_id=1, source_target_pairs={{1,0},{2,1},{3,2},{4,3},{5,4},{6,5},{7,6},{0,7},{9,8},{10,9},{11,1... | collective-permute-start | bytes 416 | tf_op jit(solution)/shard_map/ppermute | solution.py:16
  31.3 5.7 collective-permute-start.4
  34.9 3.1 collective-permute-start.5
  38.1 14.5 %collective-permute-start.6 = (bf16[32,34,1]{2,0,1:T(8,128)(2,1)S(1)}, bf16[32,34,1]{2,0,1:T(8,128)(2,1)S(1)}, u32[]{:S(2)}, u32[]{:S(2)}) collective-permute-start(bf16[32,34,1]{2,0,1:T(8,128)(2,1)S(1)} %get-tuple-element.15), channel_id=1, source_target_pairs={{0,1},{1,2},{2,3},{3,4},{4,5},{5,6},{6,7},{7,0},{8,9},{9,10},{10,1... | collective-permute-start | bytes 6536 | tf_op jit(solution)/shard_map/ppermute | solution.py:15
  40.0 17.5 %collective-permute-start.7 = (bf16[32,34,1]{2,0,1:T(8,128)(2,1)S(1)}, bf16[32,34,1]{2,0,1:T(8,128)(2,1)S(1)}, u32[]{:S(2)}, u32[]{:S(2)}) collective-permute-start(bf16[32,34,1]{2,0,1:T(8,128)(2,1)S(1)} %get-tuple-element.16), channel_id=1, source_target_pairs={{1,0},{2,1},{3,2},{4,3},{5,4},{6,5},{7,6},{0,7},{9,8},{10,9},{11,1... | collective-permute-start | bytes 6536 | tf_op jit(solution)/shard_map/ppermute | solution.py:16
  59.2 0.7 copy-start.2
  59.2 0.7 copy-start.4
  59.2 0.7 copy-start.5
  63.3 5.2 collective-permute-start.9
  66.1 3.1 collective-permute-start.8
  69.4 11.6 %collective-permute-start.10 = (bf16[32,34,1]{2,0,1:T(8,128)(2,1)S(1)}, bf16[32,34,1]{2,0,1:T(8,128)(2,1)S(1)}, u32[]{:S(2)}, u32[]{:S(2)}) collective-permute-start(bf16[32,34,1]{2,0,1:T(8,128)(2,1)S(1)} %get-tuple-element.11), channel_id=1, source_target_pairs={{1,0},{2,1},{3,2},{4,3},{5,4},{6,5},{7,6},{0,7},{9,8},{10,9},{11,1... | collective-permute-start | bytes 6536 | tf_op jit(solution)/shard_map/ppermute | solution.py:16
  75.0 13.3 %collective-permute-start.11 = (bf16[32,34,1]{2,0,1:T(8,128)(2,1)S(1)}, bf16[32,34,1]{2,0,1:T(8,128)(2,1)S(1)}, u32[]{:S(2)}, u32[]{:S(2)}) collective-permute-start(bf16[32,34,1]{2,0,1:T(8,128)(2,1)S(1)} %get-tuple-element.12), channel_id=1, source_target_pairs={{0,1},{1,2},{2,3},{3,4},{4,5},{5,6},{6,7},{7,0},{8,9},{9,10},{10,1... | collective-permute-start | bytes 6536 | tf_op jit(solution)/shard_map/ppermute | solution.py:15
  95.4 6.6 %copy-start.3 = (f32[3,3,32]{2,1,0:T(4,128)S(1)}, f32[3,3,32]{2,1,0:T(4,128)}, u32[]{:S(2)}) copy-start(f32[3,3,32]{2,1,0:T(4,128)} %param.10) | copy-start | bytes 3460
  95.8 6.6 %collective-permute-start.13 = (f32[32,1,128]{2,0,1:T(8,128)S(1)}, f32[32,1,128]{2,0,1:T(8,128)S(1)}, u32[]{:S(2)}, u32[]{:S(2)}) collective-permute-start(f32[32,1,128]{2,0,1:T(8,128)S(1)} %get-tuple-element.8), channel_id=1, source_target_pairs={{8,0},{0,8},{9,1},{1,9},{10,2},{2,10},{11,3},{3,11},{12,4},{4,12},... | collective-permute-start | bytes 49160 | tf_op jit(solution)/shard_map/ppermute | solution.py:16
  99.0 3.4 collective-permute-start.12
  103.1 9.1 %collective-permute-start.14 = (f32[32,34,1]{1,0,2:T(8,128)S(1)}, f32[32,34,1]{1,0,2:T(8,128)S(1)}, u32[]{:S(2)}, u32[]{:S(2)}) collective-permute-start(f32[32,34,1]{1,0,2:T(8,128)S(1)} %copy.33), channel_id=1, source_target_pairs={{1,0},{2,1},{3,2},{4,3},{5,4},{6,5},{7,6},{0,7},{9,8},{10,9},{11,1... | collective-permute-start | bytes 13064 | tf_op jit(solution)/shard_map/ppermute | solution.py:16
  109.5 8.1 %collective-permute-start.15 = (f32[32,34,1]{1,0,2:T(8,128)S(1)}, f32[32,34,1]{1,0,2:T(8,128)S(1)}, u32[]{:S(2)}, u32[]{:S(2)}) collective-permute-start(f32[32,34,1]{1,0,2:T(8,128)S(1)} %copy.35), channel_id=1, source_target_pairs={{0,1},{1,2},{2,3},{3,4},{4,5},{5,6},{6,7},{7,0},{8,9},{9,10},{10,1... | collective-permute-start | bytes 13064 | tf_op jit(solution)/shard_map/ppermute | solution.py:15
Sparse Core Ops, SparseCore 0:
  102.5 461.0 all-reduce.1
where the time goes:
time: 573 us
  waiting for transfers between devices  469 us (82%)
  starting transfers between devices  59.9 us (10%)
  matrix products  16.1 us (3%)
  between operations  14.6 us (3%)
  local copies, waits for them, and re-layouts  7.8 us (1%)
    psum x1, waiting for transfers between devices, on_device(): summed_grads = lax.psum(stacked, ('dp', 'gx', 'gy'))  442 us
    ppermute x8, starting transfers between devices, extended(): after = lax.ppermute(initial, axis, down)  36 us
    ppermute x8, starting transfers between devices, extended(): before = lax.ppermute(last, axis, up)  23.8 us
    ppermute x8, waiting for transfers between devices, extended(): before = lax.ppermute(last, axis, up)  17.5 us
  transfers between devices with their start and end apart: 17, of which 9 were waited for; matrix products, arithmetic and copies ran while one was open for 2% of the time, Pallas kernels for 0%

commit v1 on v0

--- a/solution.py
+++ b/solution.py
@@ -3,6 +3,11 @@
 import jax.numpy as jnp
 from jax import lax
 from jax.sharding import PartitionSpec as P
+
+
+def axis_by_axis(value_2, inner_axis, outer_axis):
+    half = lax.psum(value_2, inner_axis)
+    return lax.psum(half, outer_axis)
 
 
 def extended(value, sides, width):
@@ -114,7 +119,7 @@
         * grad_scale
     )
     stacked = jnp.concatenate([layer_grads[None], partial_prior], axis=0)
-    summed_grads = lax.psum(stacked, ("dp", "gx", "gy"))
+    summed_grads = axis_by_axis(stacked, ("gx", "gy"), "dp")
     return (coupled[None], field_grad[None], summed_grads)
 
 

time: 573 us -> 532 us (0.928)
  the two profiles are of different devices: /device:TPU:1 before, /device:TPU:2 now
where the time goes in v1:
time: 532 us; the launch traced here: 531 us
  waiting for transfers between devices  435 us (82%)
  starting transfers between devices  50.6 us (10%)
  matrix products  16.1 us (3%)
  between operations  14.6 us (3%)
  local copies, waits for them, and re-layouts  8.54 us (2%)
  other arithmetic  5.95 us (1%)
    psum x1, waiting for transfers between devices, axis_by_axis(): return lax.psum(half, outer_axis)  258 us
    psum x1, waiting for transfers between devices, axis_by_axis(): half = lax.psum(value_2, inner_axis)  146 us
    ppermute x8, starting transfers between devices, extended(): after = lax.ppermute(initial, axis, down)  28.7 us
    ppermute x8, starting transfers between devices, extended(): before = lax.ppermute(last, axis, up)  21.6 us
    ppermute x8, waiting for transfers between devices, extended(): before = lax.ppermute(last, axis, up)  19.8 us
    ppermute x8, waiting for transfers between devices, extended(): after = lax.ppermute(initial, axis, down)  11.3 us
  transfers between devices with their start and end apart: 18, of which 10 were waited for; matrix products, arithmetic and copies ran while one was open for 3% of the time, Pallas kernels for 0%

profile of v1, /device:TPU:2, one launch (start us, length us, event | category | flops | bytes accessed | tf_op | source)
XLA Modules:
  0.0 530.8 jit_solution(15385120740991326324)
XLA Ops:
  7.2 0.7 bitcast_multiply_fusion.6
  8.0 1.9 collective-permute-start
  9.9 2.4 collective-permute-start.1
  12.3 0.8 slice_bitcast_fusion.8
  13.2 1.3 copy.81
  14.6 5.1 collective-permute-start.2
  19.7 3.1 collective-permute-start.3
  22.8 4.0 collective-permute-done.3
  27.4 1.9 collective-permute-start.4
  29.4 2.4 collective-permute-start.5
  32.8 4.1 collective-permute-start.6
  36.8 4.2 collective-permute-start.7
  41.4 7.8 %collective-permute-done.6 = bf16[32,34,1]{2,0,1:T(8,128)(2,1)S(1)} collective-permute-done((bf16[32,34,1]{2,0,1:T(8,128)(2,1)S(1)}, bf16[32,34,1]{2,0,1:T(8,128)(2,1)S(1)}, u32[]{:S(2)}, u32[]{:S(2)}) %collective-permute-start.6) | collective-permute-done | bytes 2208 | tf_op jit(solution)/shard_map/ppermute | solution.py:20
  49.2 2.7 collective-permute-done.7
  57.7 1.9 collective-permute-start.9
  59.6 2.4 collective-permute-start.8
  63.0 6.5 %collective-permute-start.10 = (bf16[32,34,1]{2,0,1:T(8,128)(2,1)S(1)}, bf16[32,34,1]{2,0,1:T(8,128)(2,1)S(1)}, u32[]{:S(2)}, u32[]{:S(2)}) collective-permute-start(bf16[32,34,1]{2,0,1:T(8,128)(2,1)S(1)} %get-tuple-element.11), channel_id=1, source_target_pairs={{1,0},{2,1},{3,2},{4,3},{5,4},{6,5},{7,6},{0,7},{9,8},{10,9},{11,1... | collective-permute-start | bytes 6536 | tf_op jit(solution)/shard_map/ppermute | solution.py:21
  69.5 1.9 collective-permute-start.11
  72.0 3.9 collective-permute-done.10
  75.9 6.5 %collective-permute-done.11 = bf16[32,34,1]{2,0,1:T(8,128)(2,1)S(1)} collective-permute-done((bf16[32,34,1]{2,0,1:T(8,128)(2,1)S(1)}, bf16[32,34,1]{2,0,1:T(8,128)(2,1)S(1)}, u32[]{:S(2)}, u32[]{:S(2)}) %collective-permute-start.11) | collective-permute-done | bytes 2208 | tf_op jit(solution)/shard_map/ppermute | solution.py:20
  89.9 1.9 collective-permute-start.13
  91.8 2.4 collective-permute-start.12
  94.2 1.0 pad_maximum_fusion.1
  96.6 6.2 %collective-permute-start.14 = (f32[32,34,1]{1,0,2:T(8,128)S(1)}, f32[32,34,1]{1,0,2:T(8,128)S(1)}, u32[]{:S(2)}, u32[]{:S(2)}) collective-permute-start(f32[32,34,1]{1,0,2:T(8,128)S(1)} %copy.33), channel_id=1, source_target_pairs={{1,0},{2,1},{3,2},{4,3},{5,4},{6,5},{7,6},{0,7},{9,8},{10,9},{11,1... | collective-permute-start | bytes 13064 | tf_op jit(solution)/shard_map/ppermute | solution.py:21
  103.3 1.9 collective-permute-start.15
  106.6 5.1 collective-permute-done.15
  111.8 1.4 copy.36
  113.1 1.4 pad_maximum_fusion
  116.0 145.8 %all-reduce.3.cloned.1.call-done = f32[24,9568]{1,0:T(8,128)} async-done(((f32[24,9568]{1,0:T(8,128)}), f32[24,9568]{1,0:T(8,128)}) %all-reduce.3.cloned.1.call-update) | async-done | bytes 918544 | tf_op jit(solution)/shard_map/psum | solution.py:9
  263.1 0.6 fusion.86
  263.7 258.1 %all-reduce.5.cloned.1.call-done = f32[24,9568]{1,0:T(8,128)} async-done(((f32[24,9568]{1,0:T(8,128)}), f32[24,9568]{1,0:T(8,128)}) %all-reduce.5.cloned.1.call-update) | async-done | bytes 918544 | tf_op jit(solution)/shard_map/psum | solution.py:10
  521.8 2.2 copy.92
  (104 shorter events, 22.5 us)
Async XLA Ops:
  7.2 46.8 %copy-start = (bf16[2,32]{1,0:T(2,128)(2,1)S(1)}, bf16[2,32]{1,0:T(2,128)(2,1)}, u32[]{:S(2)}) copy-start(bf16[2,32]{1,0:T(2,128)(2,1)} %param.12) | copy-start | bytes 388
  7.2 254.6 %all-reduce.3.cloned.1.call-start = ((), (), s32[]{:S(2)}) async-start(), calls=%async_computation | async-start | bytes 1843200 | tf_op jit(solution)/shard_map/psum | solution.py:9
  8.0 6.5 %collective-permute-start = (f32[1,128]{1,0:T(1,128)S(1)}, f32[1,128]{1,0:T(1,128)S(1)}, u32[]{:S(2)}, u32[]{:S(2)}) collective-permute-start(f32[1,128]{1,0:T(1,128)S(1)} %get-tuple-element.38), channel_id=1, source_target_pairs={{0,8},{8,0},{1,9},{9,1},{2,10},{10,2},{3,11},{11,3},{4,12},{12,4},... | collective-permute-start | bytes 1544 | tf_op jit(solution)/shard_map/ppermute | solution.py:20
  9.9 4.6 collective-permute-start.1
  13.2 18.6 %copy-start.1 = (bf16[3,3,32,32]{3,2,1,0:T(8,128)(2,1)S(1)}, bf16[3,3,32,32]{3,2,1,0:T(8,128)(2,1)}, u32[]{:S(2)}) copy-start(bf16[3,3,32,32]{3,2,1,0:T(8,128)(2,1)} %param.11) | copy-start | bytes 55300
  14.6 8.3 %collective-permute-start.2 = (f32[34,1]{1,0:T(8,128)S(1)}, f32[34,1]{1,0:T(8,128)S(1)}, u32[]{:S(2)}, u32[]{:S(2)}) collective-permute-start(f32[34,1]{1,0:T(8,128)S(1)} %get-tuple-element.32), channel_id=1, source_target_pairs={{0,1},{1,2},{2,3},{3,4},{4,5},{5,6},{6,7},{7,0},{8,9},{9,10},{10,1... | collective-permute-start | bytes 416 | tf_op jit(solution)/shard_map/ppermute | solution.py:20
  19.7 7.2 %collective-permute-start.3 = (f32[34,1]{1,0:T(8,128)S(1)}, f32[34,1]{1,0:T(8,128)S(1)}, u32[]{:S(2)}, u32[]{:S(2)}) collective-permute-start(f32[34,1]{1,0:T(8,128)S(1)} %get-tuple-element.33), channel_id=1, source_target_pairs={{1,0},{2,1},{3,2},{4,3},{5,4},{6,5},{7,6},{0,7},{9,8},{10,9},{11,1... | collective-permute-start | bytes 416 | tf_op jit(solution)/shard_map/ppermute | solution.py:21
  27.4 4.6 collective-permute-start.4
  29.4 3.2 collective-permute-start.5
  32.8 16.4 %collective-permute-start.6 = (bf16[32,34,1]{2,0,1:T(8,128)(2,1)S(1)}, bf16[32,34,1]{2,0,1:T(8,128)(2,1)S(1)}, u32[]{:S(2)}, u32[]{:S(2)}) collective-permute-start(bf16[32,34,1]{2,0,1:T(8,128)(2,1)S(1)} %get-tuple-element.15), channel_id=1, source_target_pairs={{0,1},{1,2},{2,3},{3,4},{4,5},{5,6},{6,7},{7,0},{8,9},{9,10},{10,1... | collective-permute-start | bytes 6536 | tf_op jit(solution)/shard_map/ppermute | solution.py:20
  36.8 15.1 %collective-permute-start.7 = (bf16[32,34,1]{2,0,1:T(8,128)(2,1)S(1)}, bf16[32,34,1]{2,0,1:T(8,128)(2,1)S(1)}, u32[]{:S(2)}, u32[]{:S(2)}) collective-permute-start(bf16[32,34,1]{2,0,1:T(8,128)(2,1)S(1)} %get-tuple-element.16), channel_id=1, source_target_pairs={{1,0},{2,1},{3,2},{4,3},{5,4},{6,5},{7,6},{0,7},{9,8},{10,9},{11,1... | collective-permute-start | bytes 6536 | tf_op jit(solution)/shard_map/ppermute | solution.py:21
  53.6 0.7 copy-start.2
  53.6 0.7 copy-start.4
  53.6 0.7 copy-start.5
  57.7 4.8 collective-permute-start.9
  59.6 3.2 collective-permute-start.8
  63.0 12.9 %collective-permute-start.10 = (bf16[32,34,1]{2,0,1:T(8,128)(2,1)S(1)}, bf16[32,34,1]{2,0,1:T(8,128)(2,1)S(1)}, u32[]{:S(2)}, u32[]{:S(2)}) collective-permute-start(bf16[32,34,1]{2,0,1:T(8,128)(2,1)S(1)} %get-tuple-element.11), channel_id=1, source_target_pairs={{1,0},{2,1},{3,2},{4,3},{5,4},{6,5},{7,6},{0,7},{9,8},{10,9},{11,1... | collective-permute-start | bytes 6536 | tf_op jit(solution)/shard_map/ppermute | solution.py:21
  69.5 12.9 %collective-permute-start.11 = (bf16[32,34,1]{2,0,1:T(8,128)(2,1)S(1)}, bf16[32,34,1]{2,0,1:T(8,128)(2,1)S(1)}, u32[]{:S(2)}, u32[]{:S(2)}) collective-permute-start(bf16[32,34,1]{2,0,1:T(8,128)(2,1)S(1)} %get-tuple-element.12), channel_id=1, source_target_pairs={{0,1},{1,2},{2,3},{3,4},{4,5},{5,6},{6,7},{7,0},{8,9},{9,10},{10,1... | collective-permute-start | bytes 6536 | tf_op jit(solution)/shard_map/ppermute | solution.py:20
  89.5 5.8 %copy-start.3 = (f32[3,3,32]{2,1,0:T(4,128)S(1)}, f32[3,3,32]{2,1,0:T(4,128)}, u32[]{:S(2)}) copy-start(f32[3,3,32]{2,1,0:T(4,128)} %param.10) | copy-start | bytes 3460
  89.9 6.0 %collective-permute-start.13 = (f32[32,1,128]{2,0,1:T(8,128)S(1)}, f32[32,1,128]{2,0,1:T(8,128)S(1)}, u32[]{:S(2)}, u32[]{:S(2)}) collective-permute-start(f32[32,1,128]{2,0,1:T(8,128)S(1)} %get-tuple-element.8), channel_id=1, source_target_pairs={{8,0},{0,8},{9,1},{1,9},{10,2},{2,10},{11,3},{3,11},{12,4},{4,12},... | collective-permute-start | bytes 49160 | tf_op jit(solution)/shard_map/ppermute | solution.py:21
  91.8 4.1 collective-permute-start.12
  95.7 426.1 %all-reduce.5.cloned.1.call-start = ((), (), s32[]{:S(2)}) async-start(), calls=%async_computation.1 | async-start | bytes 1843200 | tf_op jit(solution)/shard_map/psum | solution.py:10
  96.6 9.4 %collective-permute-start.14 = (f32[32,34,1]{1,0,2:T(8,128)S(1)}, f32[32,34,1]{1,0,2:T(8,128)S(1)}, u32[]{:S(2)}, u32[]{:S(2)}) collective-permute-start(f32[32,34,1]{1,0,2:T(8,128)S(1)} %copy.33), channel_id=1, source_target_pairs={{1,0},{2,1},{3,2},{4,3},{5,4},{6,5},{7,6},{0,7},{9,8},{10,9},{11,1... | collective-permute-start | bytes 13064 | tf_op jit(solution)/shard_map/ppermute | solution.py:21
  103.3 8.5 %collective-permute-start.15 = (f32[32,34,1]{1,0,2:T(8,128)S(1)}, f32[32,34,1]{1,0,2:T(8,128)S(1)}, u32[]{:S(2)}, u32[]{:S(2)}) collective-permute-start(f32[32,34,1]{1,0,2:T(8,128)S(1)} %copy.35), channel_id=1, source_target_pairs={{0,1},{1,2},{2,3},{3,4},{4,5},{5,6},{6,7},{7,0},{8,9},{9,10},{10,1... | collective-permute-start | bytes 13064 | tf_op jit(solution)/shard_map/ppermute | solution.py:20
Sparse Core Ops, SparseCore 0:
  95.8 165.9 all-reduce.2
  264.9 256.7 all-reduce.4
